TPU v7x, 32 devices: a whole 2x2x4 slice. The times are simulated.
32 devices in a mesh: groups: 2 (over x), section: 1, expert: 16 (over z, y, core).
Axes of the slice: x: 2, y: 2, z: 4, core: 2. Of those that a mesh axis runs over, the one named last changes fastest.
Arguments:
- inputs: bfloat16 [2, 512, 2048], P(None, ('groups', 'expert')), parts along dimension 1, may hold values from -6 to 6
- routes: int32 [2, 2, 512, 8], P('section', None, ('groups', 'expert')), parts along dimension 2, may hold values from 0 to 15, all different within a row; in each aligned block of 16 rows (0 to 15, 16 to 31, ..., all dimensions but the last counted through in order) at most 16 rows name the same one
- norm_gain: float32 [2, 2048], P('section'), may hold values from 0.1 to 1.9
- w_gate_up: bfloat16 [2, 16, 2048, 1536], P('section', 'expert'), may hold values from -0.125 to 0.125
- w_down: bfloat16 [2, 16, 768, 2048], P('section', 'expert'), may hold values from -0.4375 to 0.4375
Outputs:
- outputs: bfloat16 [2, 2, 512, 2048], P('section', None, ('groups', 'expert')), parts along dimension 2
There are 2 independent parts, one for each index of `groups`. A program takes and returns all parts, laid end to end along the dimension named above; an argument that names none is the same for every part. Nothing has to cross between parts.
Inputs may be any that keep to these rules, and one draw needn't show every extreme that they name: `routes`: the 8 entries of a row differ. In each aligned block of 16 rows (the rows of one index of expert in one micro-batch of one layer) no expert is named by more than 16 rows, and some block reaches 16.
All inputs are finite; a program needn't handle non-finite values.
Results may differ from a plain program's by a relative error of at most 0.0055.
Values may be sent and summed in bfloat16 or wider, within the bound.
A program may use at most 64 MiB of HBM per device.

v0:
```python
import jax
import jax.numpy as jnp
from jax import lax
from jax.sharding import PartitionSpec as P

eps = 1e-06


def from_behind(value, axis, steps):
    count = lax.axis_size(axis)
    initial, last = (max(0, -steps), min(count, count - steps))
    return lax.ppermute(value, axis, [(source, source + steps) for source in range(initial, last)])


def expert_rows(rows, gate_up, down_proj):
    hidden_size = down_proj.shape[0]
    joined = jnp.dot(rows, gate_up, preferred_element_type=jnp.float32)
    hidden = (jax.nn.silu(joined[:, :hidden_size]) * joined[:, hidden_size:]).astype(jnp.bfloat16)
    return jnp.dot(hidden, down_proj, preferred_element_type=jnp.float32).astype(jnp.bfloat16)


def run_experts(received, gate_up, down_proj):
    flat = received.reshape(-1, received.shape[2])
    done = expert_rows(flat, gate_up, down_proj)
    return done.reshape(received.shape)


def moe_layer(current, layer_routes, gain_row, gate_up, down_proj, experts, capacity):
    tokens, features = current.shape
    widened = current.astype(jnp.float32)
    scale_inv = lax.rsqrt(jnp.mean(widened * widened, axis=-1, keepdims=True) + eps)
    normed = (widened * scale_inv * gain_row).astype(jnp.bfloat16)
    expert_ids = jnp.arange(experts, dtype=jnp.int32)
    onehot = (layer_routes[:, :, None] == expert_ids[None, None, :]).astype(jnp.int32)
    counted = jnp.sum(onehot, axis=1)
    before = jnp.cumsum(counted, axis=0) - counted
    slot_of = jnp.sum(onehot * (expert_ids[None, None, :] * capacity + before[:, None, :]), axis=2)
    slot_ids = jnp.arange(experts * capacity, dtype=jnp.int32)
    placing = jnp.sum(
        (slot_ids[:, None, None] == slot_of[None, :, :]).astype(jnp.int32), axis=2
    ).astype(jnp.bfloat16)
    outgoing = jnp.dot(placing, normed, preferred_element_type=jnp.float32).astype(jnp.bfloat16)
    outgoing = outgoing.reshape(experts, capacity, features)
    results = run_experts(
        lax.all_to_all(outgoing, "expert", split_axis=0, concat_axis=0, tiled=True),
        gate_up,
        down_proj,
    )
    returned = lax.all_to_all(results, "expert", split_axis=0, concat_axis=0, tiled=True).reshape(
        experts * capacity, features
    )
    combined = (
        jnp.einsum("it,id->td", placing, returned, preferred_element_type=jnp.float32) * 0.125
    )
    return (widened + combined).astype(jnp.bfloat16)


def on_device(inputs, routes, norm_gain, w_gate_up, w_down):
    experts = lax.axis_size("expert")
    sections = lax.axis_size("section")
    batches, tokens, features = inputs.shape
    top_k = routes.shape[3]
    capacity = min(tokens, 2 * tokens * top_k // experts)
    if sections == 1:
        layers_out = []
        previous = [inputs[batch_no] for batch_no in range(batches)]
        for layer_no in range(routes.shape[0]):
            current_layer = []
            for batch_no in range(batches):
                current_layer.append(
                    moe_layer(
                        previous[batch_no],
                        routes[layer_no, batch_no],
                        norm_gain[layer_no],
                        w_gate_up[layer_no, 0],
                        w_down[layer_no, 0],
                        experts,
                        capacity,
                    )
                )
            layers_out.append(jnp.stack(current_layer))
            previous = current_layer
        return jnp.stack(layers_out)
    segment_no = lax.axis_index("section")
    layer_routes = routes[0]
    gain_row = norm_gain[0]
    gate_up = w_gate_up[0, 0]
    down_proj = w_down[0, 0]
    handed = jnp.zeros((tokens, features), jnp.bfloat16)
    finished = []
    for turn_no in range(batches + 1):
        if turn_no < batches:
            fresh_rows = inputs[turn_no]
        else:
            fresh_rows = jnp.zeros((tokens, features), jnp.bfloat16)
        current = jnp.where(segment_no == 0, fresh_rows, handed)
        batch_pick = jnp.clip(turn_no - segment_no, 0, batches - 1)
        turn_routes = lax.dynamic_index_in_dim(layer_routes, batch_pick, 0, keepdims=False)
        result = moe_layer(current, turn_routes, gain_row, gate_up, down_proj, experts, capacity)
        finished.append(result)
        if turn_no < batches:
            handed = from_behind(result, "section", 1)
    first_segment = jnp.stack(finished[:batches])
    second_segment = jnp.stack(finished[1:])
    return jnp.where(segment_no == 0, first_segment, second_segment)[None]


def solution(mesh):
    placed = (
        P(None, ("groups", "expert"), None),
        P("section", None, ("groups", "expert"), None),
        P("section", None),
        P("section", "expert", None, None),
        P("section", "expert", None, None),
    )
    return jax.shard_map(
        on_device,
        mesh=mesh,
        in_specs=placed,
        out_specs=P("section", None, ("groups", "expert"), None),
        check_vma=False,
    )
```

profile of v0, /device:TPU:0, one launch (start us, length us, event | category | flops | bytes accessed | tf_op | source)
XLA Modules:
  0.0 245.7 jit_solution(4959592539766121548)
XLA Ops:
  0.0 0.0 copy-start
  0.0 0.8 slice_bitcast_fusion.1
  0.8 0.1 copy.10
  0.9 0.1 convert_reduce_fusion.7
  1.0 0.1 copy.11
  1.0 0.1 convert_reduce_fusion.6
  1.2 0.1 copy.12
  1.3 0.1 convert_reduce_fusion.5
  1.4 0.1 copy.13
  1.5 0.1 convert_reduce_fusion.4
  1.6 0.7 select_reduce_fusion.2
  2.3 0.1 convert_reduce_fusion.3
  2.4 1.0 fusion.64
  3.4 0.8 fusion.98
  4.3 2.3 convolution_convert_fusion.3
  6.6 7.4 %all-to-all-start = ((bf16[16,16,2048]{2,1,0:T(8,128)(2,1)}), bf16[16,16,2048]{2,1,0:T(8,128)(2,1)S(1)}, u32[]{:S(2)}, u32[]{:S(2)}) async-start(bf16[16,16,2048]{2,1,0:T(8,128)(2,1)} %bitcast.4), calls=%async_computation | async-start | bytes 2097152 | tf_op jit(solution)/shard_map/all_to_all | solution.py:45
  14.0 0.1 convert_reduce_fusion.2
  14.2 0.0 copy-done
  14.2 1.5 convolution_convert_fusion.2
  15.6 21.3 %all-to-all-done = bf16[16,16,2048]{2,1,0:T(8,128)(2,1)S(1)} async-done(((bf16[16,16,2048]{2,1,0:T(8,128)(2,1)}), bf16[16,16,2048]{2,1,0:T(8,128)(2,1)S(1)}, u32[]{:S(2)}, u32[]{:S(2)}) %all-to-all-start) | async-done | bytes 1048608 | tf_op jit(solution)/shard_map/all_to_all | solution.py:45
  36.9 6.8 %all-to-all-start.2 = ((bf16[16,16,2048]{2,1,0:T(8,128)(2,1)}), bf16[16,16,2048]{2,1,0:T(8,128)(2,1)S(1)}, u32[]{:S(2)}, u32[]{:S(2)}) async-start(bf16[16,16,2048]{2,1,0:T(8,128)(2,1)} %bitcast.14), calls=%async_computation.2 | async-start | bytes 2097152 | tf_op jit(solution)/shard_map/all_to_all | solution.py:45
  43.7 4.6 %fusion.6 = f32[256,1536]{1,0:T(8,128)S(1)} fusion(bf16[256,2048]{1,0:T(8,128)(2,1)S(1)} %bitcast.95, bf16[2,1,2048,1536]{3,2,1,0:T(8,128)(2,1)} %param.8), kind=kOutput, calls=%fused_computation.6 | convolution fusion | flops 1610612736 | bytes 8912896 | tf_op jit(solution)/shard_map/dot_general | solution.py:17
  48.3 4.0 %fusion.24 = bf16[256,2048]{1,0:T(8,128)(2,1)} fusion(bf16[2,1,768,2048]{3,2,1,0:T(8,128)(2,1)} %param.9, f32[256,1536]{1,0:T(8,128)S(1)} %fusion.6), kind=kOutput, calls=%fused_computation.24 | convolution fusion | flops 807010304 | bytes 5767168 | tf_op jit(solution)/shard_map/dot_general | solution.py:19
  52.3 14.3 %all-to-all-done.2 = bf16[16,16,2048]{2,1,0:T(8,128)(2,1)S(1)} async-done(((bf16[16,16,2048]{2,1,0:T(8,128)(2,1)}), bf16[16,16,2048]{2,1,0:T(8,128)(2,1)S(1)}, u32[]{:S(2)}, u32[]{:S(2)}) %all-to-all-start.2) | async-done | bytes 1048608 | tf_op jit(solution)/shard_map/all_to_all | solution.py:45
  66.6 6.8 %all-to-all-start.1 = ((bf16[16,16,2048]{2,1,0:T(8,128)(2,1)}), bf16[16,16,2048]{2,1,0:T(8,128)(2,1)S(1)}, u32[]{:S(2)}, u32[]{:S(2)}) async-start(bf16[16,16,2048]{2,1,0:T(8,128)(2,1)} %bitcast.8), calls=%async_computation.1 | async-start | bytes 2097152 | tf_op jit(solution)/shard_map/all_to_all | solution.py:49
  73.4 4.6 %fusion.4 = f32[256,1536]{1,0:T(8,128)S(1)} fusion(bf16[256,2048]{1,0:T(8,128)(2,1)S(1)} %bitcast.96, bf16[2,1,2048,1536]{3,2,1,0:T(8,128)(2,1)} %param.8), kind=kOutput, calls=%fused_computation.4 | convolution fusion | flops 1610612736 | bytes 8912896 | tf_op jit(solution)/shard_map/dot_general | solution.py:17
  78.0 3.9 %fusion.27 = bf16[256,2048]{1,0:T(8,128)(2,1)} fusion(bf16[2,1,768,2048]{3,2,1,0:T(8,128)(2,1)} %param.9, f32[256,1536]{1,0:T(8,128)S(1)} %fusion.4), kind=kOutput, calls=%fused_computation.25 | convolution fusion | flops 807010304 | bytes 5767168 | tf_op jit(solution)/shard_map/dot_general | solution.py:19
  81.9 14.4 %all-to-all-done.1 = bf16[16,16,2048]{2,1,0:T(8,128)(2,1)S(1)} async-done(((bf16[16,16,2048]{2,1,0:T(8,128)(2,1)}), bf16[16,16,2048]{2,1,0:T(8,128)(2,1)S(1)}, u32[]{:S(2)}, u32[]{:S(2)}) %all-to-all-start.1) | async-done | bytes 1048608 | tf_op jit(solution)/shard_map/all_to_all | solution.py:49
  96.3 6.8 %all-to-all-start.3 = ((bf16[16,16,2048]{2,1,0:T(8,128)(2,1)}), bf16[16,16,2048]{2,1,0:T(8,128)(2,1)S(1)}, u32[]{:S(2)}, u32[]{:S(2)}) async-start(bf16[16,16,2048]{2,1,0:T(8,128)(2,1)} %bitcast.16), calls=%async_computation.3 | async-start | bytes 2097152 | tf_op jit(solution)/shard_map/all_to_all | solution.py:49
  103.1 0.4 select_reduce_fusion.1
  103.5 0.1 convert_reduce_fusion.1
  103.6 0.4 fusion.58
  104.0 1.5 convolution_convert_fusion.1
  105.5 20.4 %all-to-all-done.3 = bf16[16,16,2048]{2,1,0:T(8,128)(2,1)S(1)} async-done(((bf16[16,16,2048]{2,1,0:T(8,128)(2,1)}), bf16[16,16,2048]{2,1,0:T(8,128)(2,1)S(1)}, u32[]{:S(2)}, u32[]{:S(2)}) %all-to-all-start.3) | async-done | bytes 1048608 | tf_op jit(solution)/shard_map/all_to_all | solution.py:49
  126.0 6.8 %all-to-all-start.4 = ((bf16[16,16,2048]{2,1,0:T(8,128)(2,1)}), bf16[16,16,2048]{2,1,0:T(8,128)(2,1)S(1)}, u32[]{:S(2)}, u32[]{:S(2)}) async-start(bf16[16,16,2048]{2,1,0:T(8,128)(2,1)} %bitcast.22), calls=%async_computation.4 | async-start | bytes 2097152 | tf_op jit(solution)/shard_map/all_to_all | solution.py:45
  132.8 0.4 select_reduce_fusion
  133.2 0.1 convert_reduce_fusion
  133.3 0.4 fusion.61
  133.7 1.5 convolution_convert_fusion
  135.2 20.5 %all-to-all-done.4 = bf16[16,16,2048]{2,1,0:T(8,128)(2,1)S(1)} async-done(((bf16[16,16,2048]{2,1,0:T(8,128)(2,1)}), bf16[16,16,2048]{2,1,0:T(8,128)(2,1)S(1)}, u32[]{:S(2)}, u32[]{:S(2)}) %all-to-all-start.4) | async-done | bytes 1048608 | tf_op jit(solution)/shard_map/all_to_all | solution.py:45
  155.7 6.8 %all-to-all-start.6 = ((bf16[16,16,2048]{2,1,0:T(8,128)(2,1)}), bf16[16,16,2048]{2,1,0:T(8,128)(2,1)S(1)}, u32[]{:S(2)}, u32[]{:S(2)}) async-start(bf16[16,16,2048]{2,1,0:T(8,128)(2,1)} %bitcast.30), calls=%async_computation.6 | async-start | bytes 2097152 | tf_op jit(solution)/shard_map/all_to_all | solution.py:45
  162.5 4.6 %fusion.2 = f32[256,1536]{1,0:T(8,128)S(1)} fusion(bf16[256,2048]{1,0:T(8,128)(2,1)S(1)} %bitcast.94, bf16[2,1,2048,1536]{3,2,1,0:T(8,128)(2,1)} %param.8), kind=kOutput, calls=%fused_computation.2 | convolution fusion | flops 1610612736 | bytes 8912896 | tf_op jit(solution)/shard_map/dot_general | solution.py:17
  167.0 4.0 %fusion.30 = bf16[256,2048]{1,0:T(8,128)(2,1)} fusion(bf16[2,1,768,2048]{3,2,1,0:T(8,128)(2,1)} %param.9, f32[256,1536]{1,0:T(8,128)S(1)} %fusion.2), kind=kOutput, calls=%fused_computation.26 | convolution fusion | flops 807010304 | bytes 5767168 | tf_op jit(solution)/shard_map/dot_general | solution.py:19
  171.0 14.3 %all-to-all-done.6 = bf16[16,16,2048]{2,1,0:T(8,128)(2,1)S(1)} async-done(((bf16[16,16,2048]{2,1,0:T(8,128)(2,1)}), bf16[16,16,2048]{2,1,0:T(8,128)(2,1)S(1)}, u32[]{:S(2)}, u32[]{:S(2)}) %all-to-all-start.6) | async-done | bytes 1048608 | tf_op jit(solution)/shard_map/all_to_all | solution.py:45
  185.4 6.8 %all-to-all-start.5 = ((bf16[16,16,2048]{2,1,0:T(8,128)(2,1)}), bf16[16,16,2048]{2,1,0:T(8,128)(2,1)S(1)}, u32[]{:S(2)}, u32[]{:S(2)}) async-start(bf16[16,16,2048]{2,1,0:T(8,128)(2,1)} %bitcast.26), calls=%async_computation.5 | async-start | bytes 2097152 | tf_op jit(solution)/shard_map/all_to_all | solution.py:49
  192.2 4.6 %fusion = f32[256,1536]{1,0:T(8,128)S(1)} fusion(bf16[256,2048]{1,0:T(8,128)(2,1)S(1)} %bitcast.97, bf16[2,1,2048,1536]{3,2,1,0:T(8,128)(2,1)} %param.8), kind=kOutput, calls=%fused_computation | convolution fusion | flops 1610612736 | bytes 8912896 | tf_op jit(solution)/shard_map/dot_general | solution.py:17
  196.7 3.9 %fusion.33 = bf16[256,2048]{1,0:T(8,128)(2,1)} fusion(bf16[2,1,768,2048]{3,2,1,0:T(8,128)(2,1)} %param.9, f32[256,1536]{1,0:T(8,128)S(1)} %fusion), kind=kOutput, calls=%fused_computation.27 | convolution fusion | flops 807010304 | bytes 5767168 | tf_op jit(solution)/shard_map/dot_general | solution.py:19
  200.7 14.4 %all-to-all-done.5 = bf16[16,16,2048]{2,1,0:T(8,128)(2,1)S(1)} async-done(((bf16[16,16,2048]{2,1,0:T(8,128)(2,1)}), bf16[16,16,2048]{2,1,0:T(8,128)(2,1)S(1)}, u32[]{:S(2)}, u32[]{:S(2)}) %all-to-all-start.5) | async-done | bytes 1048608 | tf_op jit(solution)/shard_map/all_to_all | solution.py:49
  215.0 6.8 %all-to-all-start.7 = ((bf16[16,16,2048]{2,1,0:T(8,128)(2,1)}), bf16[16,16,2048]{2,1,0:T(8,128)(2,1)S(1)}, u32[]{:S(2)}, u32[]{:S(2)}) async-start(bf16[16,16,2048]{2,1,0:T(8,128)(2,1)} %bitcast.32), calls=%async_computation.7 | async-start | bytes 2097152 | tf_op jit(solution)/shard_map/all_to_all | solution.py:49
  221.9 0.3 fusion.45
  222.1 22.6 %all-to-all-done.7 = bf16[16,16,2048]{2,1,0:T(8,128)(2,1)S(1)} async-done(((bf16[16,16,2048]{2,1,0:T(8,128)(2,1)}), bf16[16,16,2048]{2,1,0:T(8,128)(2,1)S(1)}, u32[]{:S(2)}, u32[]{:S(2)}) %all-to-all-start.7) | async-done | bytes 1048608 | tf_op jit(solution)/shard_map/all_to_all | solution.py:49
  244.7 0.3 fusion.44
  245.0 0.7 pad_maximum_fusion
  (11 shorter events, 0.2 us)
Async XLA Ops:
  0.0 14.2 %copy-start = (bf16[2,16,2048]{2,1,0:T(8,128)(2,1)S(1)}, bf16[2,16,2048]{2,1,0:T(8,128)(2,1)}, u32[]{:S(2)}) copy-start(bf16[2,16,2048]{2,1,0:T(8,128)(2,1)} %param.5) | copy-start | bytes 393220
  6.6 30.3 %all-to-all-start = ((bf16[16,16,2048]{2,1,0:T(8,128)(2,1)}), bf16[16,16,2048]{2,1,0:T(8,128)(2,1)S(1)}, u32[]{:S(2)}, u32[]{:S(2)}) async-start(bf16[16,16,2048]{2,1,0:T(8,128)(2,1)} %bitcast.4), calls=%async_computation | async-start | bytes 2097152 | tf_op jit(solution)/shard_map/all_to_all | solution.py:45
  36.9 29.7 %all-to-all-start.2 = ((bf16[16,16,2048]{2,1,0:T(8,128)(2,1)}), bf16[16,16,2048]{2,1,0:T(8,128)(2,1)S(1)}, u32[]{:S(2)}, u32[]{:S(2)}) async-start(bf16[16,16,2048]{2,1,0:T(8,128)(2,1)} %bitcast.14), calls=%async_computation.2 | async-start | bytes 2097152 | tf_op jit(solution)/shard_map/all_to_all | solution.py:45
  66.6 29.7 %all-to-all-start.1 = ((bf16[16,16,2048]{2,1,0:T(8,128)(2,1)}), bf16[16,16,2048]{2,1,0:T(8,128)(2,1)S(1)}, u32[]{:S(2)}, u32[]{:S(2)}) async-start(bf16[16,16,2048]{2,1,0:T(8,128)(2,1)} %bitcast.8), calls=%async_computation.1 | async-start | bytes 2097152 | tf_op jit(solution)/shard_map/all_to_all | solution.py:49
  96.3 29.7 %all-to-all-start.3 = ((bf16[16,16,2048]{2,1,0:T(8,128)(2,1)}), bf16[16,16,2048]{2,1,0:T(8,128)(2,1)S(1)}, u32[]{:S(2)}, u32[]{:S(2)}) async-start(bf16[16,16,2048]{2,1,0:T(8,128)(2,1)} %bitcast.16), calls=%async_computation.3 | async-start | bytes 2097152 | tf_op jit(solution)/shard_map/all_to_all | solution.py:49
  126.0 29.7 %all-to-all-start.4 = ((bf16[16,16,2048]{2,1,0:T(8,128)(2,1)}), bf16[16,16,2048]{2,1,0:T(8,128)(2,1)S(1)}, u32[]{:S(2)}, u32[]{:S(2)}) async-start(bf16[16,16,2048]{2,1,0:T(8,128)(2,1)} %bitcast.22), calls=%async_computation.4 | async-start | bytes 2097152 | tf_op jit(solution)/shard_map/all_to_all | solution.py:45
  155.7 29.7 %all-to-all-start.6 = ((bf16[16,16,2048]{2,1,0:T(8,128)(2,1)}), bf16[16,16,2048]{2,1,0:T(8,128)(2,1)S(1)}, u32[]{:S(2)}, u32[]{:S(2)}) async-start(bf16[16,16,2048]{2,1,0:T(8,128)(2,1)} %bitcast.30), calls=%async_computation.6 | async-start | bytes 2097152 | tf_op jit(solution)/shard_map/all_to_all | solution.py:45
  185.4 29.7 %all-to-all-start.5 = ((bf16[16,16,2048]{2,1,0:T(8,128)(2,1)}), bf16[16,16,2048]{2,1,0:T(8,128)(2,1)S(1)}, u32[]{:S(2)}, u32[]{:S(2)}) async-start(bf16[16,16,2048]{2,1,0:T(8,128)(2,1)} %bitcast.26), calls=%async_computation.5 | async-start | bytes 2097152 | tf_op jit(solution)/shard_map/all_to_all | solution.py:49
  215.0 29.7 %all-to-all-start.7 = ((bf16[16,16,2048]{2,1,0:T(8,128)(2,1)}), bf16[16,16,2048]{2,1,0:T(8,128)(2,1)S(1)}, u32[]{:S(2)}, u32[]{:S(2)}) async-start(bf16[16,16,2048]{2,1,0:T(8,128)(2,1)} %bitcast.32), calls=%async_computation.7 | async-start | bytes 2097152 | tf_op jit(solution)/shard_map/all_to_all | solution.py:49
where the time goes:
time: 248 us; the launch traced here: 246 us
  waiting for transfers between devices  142 us (57%)
  starting transfers between devices  54.9 us (22%)
  matrix products  42.2 us (17%)
  other arithmetic  4.27 us (2%)
    all_to_all x4, waiting for transfers between devices, moe_layer(): lax.all_to_all(results, 'expert', split_axis=0, concat_axis=0, tiled=True)  71.8 us
    all_to_all x4, waiting for transfers between devices, moe_layer(): lax.all_to_all(outgoing, 'expert', split_axis=0, concat_axis=0, tiled=True)  70.4 us
    all_to_all x4, starting transfers between devices, moe_layer(): lax.all_to_all(outgoing, 'expert', split_axis=0, concat_axis=0, tiled=True)  27.8 us
    all_to_all x4, starting transfers between devices, moe_layer(): lax.all_to_all(results, 'expert', split_axis=0, concat_axis=0, tiled=True)  27.2 us
    dot_general x4, matrix products, expert_rows(): joined = jnp.dot(rows, gate_up, preferred_element_type=jnp.float32)  18.3 us
    dot_general x4, matrix products, expert_rows(): jnp.dot(hidden, down_proj, preferred_element_type=jnp.float32)  15.8 us
    dot_general x4, matrix products, moe_layer(): jnp.dot(placing, normed, preferred_element_type=jnp.float32)  6.82 us
  transfers between devices with their start and end apart: 8, of which 8 were waited for; matrix products, arithmetic and copies ran while one was open for 17% of the time, Pallas kernels for 0%

commit v1 on v0

--- a/solution.py
+++ b/solution.py
@@ -1,6 +1,10 @@
+import functools
+
 import jax
 import jax.numpy as jnp
 from jax import lax
+from jax.experimental import pallas as pl
+from jax.experimental.pallas import tpu as pltpu
 from jax.sharding import PartitionSpec as P
 
 eps = 1e-06
@@ -104,6 +108,334 @@
     second_segment = jnp.stack(finished[1:])
     return jnp.where(segment_no == 0, first_segment, second_segment)[None]
 
+LANES = 128
+PAIR = 2
+TILE = 256
+
+
+def flat_rows(block):
+    return block.reshape(-1, block.shape[-1])
+
+
+def moe_kernel(
+    count,
+    x_ref,
+    routes_ref,
+    gain_ref,
+    gu_hbm,
+    down_hbm,
+    out_ref,
+    gu,
+    down,
+    rows,
+    hidden,
+    made,
+    from_core,
+    to_y,
+    from_y,
+    to_z,
+    from_z,
+    w_sem,
+    az_s,
+    az_r,
+    ay_s,
+    ay_r,
+    ac_s,
+    ac_r,
+    rc_s,
+    rc_r,
+    ry_s,
+    ry_r,
+    rz_s,
+    rz_r,
+):
+    layers, batches = routes_ref.shape[0], routes_ref.shape[1]
+    tokens, features = x_ref.shape[1], x_ref.shape[2]
+    units = down.shape[1]
+    depth = count // (PAIR * PAIR)
+    me = lax.axis_index("expert")
+    c = lax.rem(me, PAIR)
+    y = lax.rem(lax.div(me, PAIR), PAIR)
+    z = lax.div(me, PAIR * PAIR)
+    other_c, other_y = 1 - c, 1 - y
+
+    def expert_at(zz, yy, cc):
+        return (zz * PAIR + yy) * PAIR + cc
+
+    def z_up(k):
+        return lax.rem(z + k, depth)
+
+    def z_down(k):
+        return lax.rem(z + depth - k, depth)
+
+    core_peer = expert_at(z, y, other_c)
+    y_peer = expert_at(z, other_y, c)
+
+    def remote(src, dst, send, recv, target):
+        return pltpu.make_async_remote_copy(
+            src_ref=src,
+            dst_ref=dst,
+            send_sem=send,
+            recv_sem=recv,
+            device_id={"expert": target},
+            device_id_type=pl.DeviceIdType.MESH,
+        )
+
+    loads = []
+    for layer in range(layers):
+        for number, (source, target) in enumerate(((gu_hbm, gu), (down_hbm, down))):
+            load = pltpu.make_async_copy(
+                source.at[layer, 0], target.at[layer], w_sem.at[layer, number]
+            )
+            load.start()
+            loads.append(load)
+
+    barrier = pltpu.get_barrier_semaphore()
+    for peer in [expert_at(z_up(k), y, c) for k in range(1, depth)] + [core_peer, y_peer]:
+        pl.semaphore_signal(
+            barrier, inc=1, device_id={"expert": peer}, device_id_type=pl.DeviceIdType.MESH
+        )
+    pl.semaphore_wait(barrier, depth + 1)
+
+    sends = []
+
+    def go(copy):
+        copy.start()
+        sends.append(copy)
+
+    def slot(layer, batch):
+        return layer * batches + batch
+
+    def gather_core(s, yy, zz, number):
+        block = rows.at[s, c, yy, zz]
+        return remote(block, block, ac_s.at[s, number], ac_r.at[s, number], core_peer)
+
+    def gather_y(s, zz, number):
+        block = rows.at[s, c, y, zz]
+        return remote(block, block, ay_s.at[s, number], ay_r.at[s, number], y_peer)
+
+    def norm_send(layer, batch):
+        s = slot(layer, batch)
+        h = (x_ref[batch] if layer == 0 else out_ref[layer - 1, batch]).astype(jnp.float32)
+        scale = lax.rsqrt(jnp.mean(h * h, axis=-1, keepdims=True) + eps)
+        normed = (h * scale * gain_ref[pl.ds(layer, 1), :]).astype(jnp.bfloat16)
+        rows[s, c, y, z, :, pl.ds(0, features)] = normed
+        lanes = lax.broadcasted_iota(jnp.int32, (tokens, LANES), 1)
+        chosen = routes_ref[layer, batch]
+        named = jnp.zeros((tokens, LANES), jnp.float32)
+        for k in range(chosen.shape[1]):
+            named = named + (chosen[:, k : k + 1] == lanes).astype(jnp.float32)
+        rows[s, c, y, z, :, pl.ds(features, LANES)] = named.astype(jnp.bfloat16)
+        block = rows.at[s, c, y, z]
+        for k in range(1, depth):
+            go(remote(block, block, az_s.at[s, k - 1], az_r.at[s, k - 1], expert_at(z_up(k), y, c)))
+        go(gather_y(s, z, 0))
+        go(gather_core(s, y, z, 0))
+
+    def gather_z_done(layer, batch):
+        s = slot(layer, batch)
+        for k in range(1, depth):
+            zz = z_down(k)
+            block = rows.at[s, c, y, zz]
+            remote(block, block, az_s.at[s, k - 1], az_r.at[s, k - 1], y_peer).wait_recv()
+            go(gather_y(s, zz, k))
+            go(gather_core(s, y, zz, k))
+
+    def gather_y_done(layer, batch):
+        s = slot(layer, batch)
+        for k in range(depth):
+            zz = z_down(k)
+            block = rows.at[s, c, other_y, zz]
+            remote(block, block, ay_s.at[s, k], ay_r.at[s, k], y_peer).wait_recv()
+            go(gather_core(s, other_y, zz, depth + k))
+
+    def gather_core_done(layer, batch):
+        s = slot(layer, batch)
+        for number in range(PAIR * depth):
+            zz = z_down(number % depth)
+            block = rows.at[s, other_c, y if number < depth else other_y, zz]
+            remote(block, block, ac_s.at[s, number], ac_r.at[s, number], core_peer).wait_recv()
+
+    def compute(layer, batch):
+        s = slot(layer, batch)
+        if batch == 0:
+            for load in loads[layer * 2 : layer * 2 + 2]:
+                load.wait()
+        named = flat_rows(rows[s, :, :, :, :, pl.ds(features, LANES)]).astype(jnp.float32)
+        lanes = lax.broadcasted_iota(jnp.int32, named.shape, 1)
+        mine = jnp.sum(jnp.where(lanes == me, named, 0.0), axis=1, keepdims=True) > 0.5
+
+        def up_tile(j, carry):
+            gate_cols = pl.ds(pl.multiple_of(j * TILE, TILE), TILE)
+            up_cols = pl.ds(pl.multiple_of(units + j * TILE, TILE), TILE)
+            x = flat_rows(rows[s, :, :, :, :, pl.ds(0, features)])
+            gate = jnp.dot(x, gu[layer, :, gate_cols], preferred_element_type=jnp.float32)
+            up = jnp.dot(x, gu[layer, :, up_cols], preferred_element_type=jnp.float32)
+            value = gate / (1.0 + jnp.exp(-gate)) * up
+            hidden[:, gate_cols] = jnp.where(mine, value, 0.0).astype(jnp.bfloat16)
+            return carry
+
+        lax.fori_loop(0, units // TILE, up_tile, 0)
+
+        def down_tile(j, carry):
+            cols = pl.ds(pl.multiple_of(j * TILE, TILE), TILE)
+            result = jnp.dot(hidden[...], down[layer, :, cols], preferred_element_type=jnp.float32)
+            made[s, :, :, :, :, cols] = result.astype(jnp.bfloat16).reshape(
+                PAIR, PAIR, depth, tokens, TILE
+            )
+            return carry
+
+        lax.fori_loop(0, features // TILE, down_tile, 0)
+
+    def sum_core_copy(s, yy, number):
+        return remote(
+            made.at[s, other_c, yy],
+            from_core.at[s, yy],
+            rc_s.at[s, number],
+            rc_r.at[s, number],
+            core_peer,
+        )
+
+    def sum_core(layer, batch):
+        s = slot(layer, batch)
+        go(sum_core_copy(s, other_y, 0))
+        go(sum_core_copy(s, y, 1))
+
+    def sum_core_wait(s, yy, number):
+        block = from_core.at[s, yy]
+        remote(block, block, rc_s.at[s, number], rc_r.at[s, number], core_peer).wait_recv()
+
+    def pair_sum(s, yy, zz):
+        return made[s, c, yy, zz].astype(jnp.float32) + from_core[s, yy, zz].astype(jnp.float32)
+
+    def sum_y(layer, batch):
+        s = slot(layer, batch)
+        sum_core_wait(s, other_y, 0)
+        for k in list(range(1, depth)) + [0]:
+            zz = z_up(k)
+            to_y[s, k] = pair_sum(s, other_y, zz).astype(jnp.bfloat16)
+            go(remote(to_y.at[s, k], from_y.at[s, k], ry_s.at[s, k], ry_r.at[s, k], y_peer))
+
+    def sum_y_wait(s, k):
+        remote(from_y.at[s, k], from_y.at[s, k], ry_s.at[s, k], ry_r.at[s, k], y_peer).wait_recv()
+
+    def sum_z(layer, batch):
+        s = slot(layer, batch)
+        sum_core_wait(s, y, 1)
+        for k in range(1, depth):
+            zz = z_up(k)
+            sum_y_wait(s, k)
+            total = pair_sum(s, y, zz) + from_y[s, k].astype(jnp.float32)
+            to_z[s, k - 1] = total.astype(jnp.bfloat16)
+            go(
+                remote(
+                    to_z.at[s, k - 1],
+                    from_z.at[s, k - 1],
+                    rz_s.at[s, k - 1],
+                    rz_r.at[s, k - 1],
+                    expert_at(zz, y, c),
+                )
+            )
+
+    def finish(layer, batch):
+        s = slot(layer, batch)
+        sum_y_wait(s, 0)
+        total = pair_sum(s, y, z) + from_y[s, 0].astype(jnp.float32)
+        for k in range(depth - 1):
+            block = from_z.at[s, k]
+            remote(block, block, rz_s.at[s, k], rz_r.at[s, k], y_peer).wait_recv()
+            total = total + from_z[s, k].astype(jnp.float32)
+        h = (x_ref[batch] if layer == 0 else out_ref[layer - 1, batch]).astype(jnp.float32)
+        out_ref[layer, batch] = (h + total * 0.125).astype(jnp.bfloat16)
+
+    norm_send(0, 0)
+    gather_z_done(0, 0)
+    norm_send(0, 1)
+    gather_y_done(0, 0)
+    gather_core_done(0, 0)
+    gather_z_done(0, 1)
+    compute(0, 0)
+    sum_core(0, 0)
+    gather_y_done(0, 1)
+    gather_core_done(0, 1)
+    sum_y(0, 0)
+    compute(0, 1)
+    sum_core(0, 1)
+    sum_z(0, 0)
+    sum_y(0, 1)
+    finish(0, 0)
+    norm_send(1, 0)
+    sum_z(0, 1)
+    gather_z_done(1, 0)
+    finish(0, 1)
+    norm_send(1, 1)
+    gather_y_done(1, 0)
+    gather_core_done(1, 0)
+    gather_z_done(1, 1)
+    compute(1, 0)
+    sum_core(1, 0)
+    gather_y_done(1, 1)
+    gather_core_done(1, 1)
+    sum_y(1, 0)
+    compute(1, 1)
+    sum_core(1, 1)
+    sum_z(1, 0)
+    sum_y(1, 1)
+    finish(1, 0)
+    sum_z(1, 1)
+    finish(1, 1)
+
+    for copy in sends:
+        copy.wait_send()
+
+
+def fused_on_device(count, inputs, routes, norm_gain, w_gate_up, w_down):
+    batches, tokens, features = inputs.shape
+    layers = routes.shape[0]
+    units = w_down.shape[2]
+    slots = layers * batches
+    depth = count // (PAIR * PAIR)
+    bf16 = jnp.bfloat16
+    vmem = pl.BlockSpec(memory_space=pltpu.VMEM)
+    hbm = pl.BlockSpec(memory_space=pl.ANY)
+    dma = pltpu.SemaphoreType.DMA
+    short = max(depth - 1, 1)
+    return pl.pallas_call(
+        functools.partial(moe_kernel, count),
+        out_shape=jax.ShapeDtypeStruct((layers, batches, tokens, features), bf16),
+        in_specs=[vmem, vmem, vmem, hbm, hbm],
+        out_specs=vmem,
+        scratch_shapes=[
+            pltpu.VMEM((layers, features, 2 * units), bf16),
+            pltpu.VMEM((layers, units, features), bf16),
+            pltpu.VMEM((slots, PAIR, PAIR, depth, tokens, features + LANES), bf16),
+            pltpu.VMEM((count * tokens, units), bf16),
+            pltpu.VMEM((slots, PAIR, PAIR, depth, tokens, features), bf16),
+            pltpu.VMEM((slots, PAIR, depth, tokens, features), bf16),
+            pltpu.VMEM((slots, depth, tokens, features), bf16),
+            pltpu.VMEM((slots, depth, tokens, features), bf16),
+            pltpu.VMEM((slots, short, tokens, features), bf16),
+            pltpu.VMEM((slots, short, tokens, features), bf16),
+            dma((layers, 2)),
+            dma((slots, short)),
+            dma((slots, short)),
+            dma((slots, depth)),
+            dma((slots, depth)),
+            dma((slots, PAIR * depth)),
+            dma((slots, PAIR * depth)),
+            dma((slots, 2)),
+            dma((slots, 2)),
+            dma((slots, depth)),
+            dma((slots, depth)),
+            dma((slots, short)),
+            dma((slots, short)),
+        ],
+        compiler_params=pltpu.CompilerParams(
+            collective_id=0, has_side_effects=True, vmem_limit_bytes=60 << 20
+        ),
+        name="moe",
+    )(inputs, routes, norm_gain, w_gate_up, w_down)
+
 
 def solution(mesh):
     placed = (
@@ -113,8 +445,10 @@
         P("section", "expert", None, None),
         P("section", "expert", None, None),
     )
+    count = mesh.shape["expert"]
+    fused = mesh.shape["section"] == 1 and count % (PAIR * PAIR) == 0 and PAIR * PAIR < count <= LANES
     return jax.shard_map(
-        on_device,
+        functools.partial(fused_on_device, count) if fused else on_device,
         mesh=mesh,
         in_specs=placed,
         out_specs=P("section", None, ("groups", "expert"), None),

time: 248 us -> 89.8 us (0.36)
  waiting for transfers between devices: 142 us -> 0 us
  Pallas kernels: 0 us -> 86.5 us
  starting transfers between devices: 54.9 us -> 0 us
  matrix products: 42.2 us -> 0 us
  other arithmetic: 4.27 us -> 0 us
    all_to_all x8 -> x0, waiting for transfers between devices: 142 us -> none  [the longest x4 71.8 us: moe_layer(): lax.all_to_all(results, 'expert', split_axis=0, concat_axis=0, tiled=True)]
    pallas_call x0 -> x1, Pallas kernels: none -> 86.5 us  [fused_on_device(): pl.pallas_call(functools.partial(moe_kernel, count), out_shape=jax.ShapeD...]
    all_to_all x8 -> x0, starting transfers between devices: 54.9 us -> none  [the longest x4 27.8 us: moe_layer(): lax.all_to_all(outgoing, 'expert', split_axis=0, concat_axis=0, tiled=True)]
    dot_general x16 -> x0, matrix products: 42.2 us -> none  [the longest x4 18.3 us: expert_rows(): joined = jnp.dot(rows, gate_up, preferred_element_type=jnp.float32)]
    reduce_sum x12 -> x0, other arithmetic: 3.34 us -> none  [the longest x3 1.51 us: moe_layer(): jnp.sum(onehot * (expert_ids[None, None, :] * capacity + before[:, None,...]
    unnamed x2, local copies, waits for them, and re-layouts: 0.01 us -> 3.08 us
  transfers between devices with their start and end apart: 8 -> 0, of which waited for: 8 -> 0; matrix products, arithmetic and copies ran while one was open for 17% -> 0% of each run, Pallas kernels for 0% -> 0%
where the time goes in v1:
time: 89.8 us; the launch traced here: 89.6 us
  Pallas kernels  86.5 us (96%)
  local copies, waits for them, and re-layouts  3.08 us (3%)
    pallas_call x1, Pallas kernels, fused_on_device(): pl.pallas_call(functools.partial(moe_kernel, count), out_shape=jax.ShapeD...  86.5 us
    unnamed x2, local copies, waits for them, and re-layouts  3.08 us

profile of v1, /device:TPU:0, one launch (start us, length us, event | category | flops | bytes accessed | tf_op | source)
XLA Modules:
  0.0 89.6 jit_solution(12727551338901711297)
XLA Ops:
  0.0 1.4 %copy.6.routes_ref = s32[2,2,16,8]{3,2,1,0:T(8,128)} copy(s32[2,2,16,8]{2,3,1,0:T(8,128)} %param.6) | data formatting | bytes 4096 | tf_op args[1]
  1.4 86.5 %moe.1 = bf16[2,2,16,2048]{3,2,1,0:T(8,128)(2,1)} custom-call(bf16[2,16,2048]{2,1,0:T(8,128)(2,1)} %x_ref.1, s32[2,2,16,8]{3,2,1,0:T(8,128)} %copy.6.routes_ref, f32[2,2048]{1,0:T(2,128)} %gain_ref.1, bf16[2,1,2048,1536]{3,2,1,0:T(8,128)(2,1)} %gu_hbm.1, bf16[2,1,768,2048]{3,2,1,0:T(8,128)(2,1)} %down_hbm.1), custom_call_target="tpu_custom_call" | custom-call | tf_op jit(solution)/shard_map/moe/pallas_call | solution.py:403
  87.9 1.7 %copy.8 = bf16[2,2,16,2048]{3,2,1,0:T(8,128)(2,1)} copy(bf16[2,2,16,2048]{3,2,1,0:T(8,128)(2,1)} %moe.1) | data formatting | bytes 524288

commit v2 on v1

--- a/solution.py
+++ b/solution.py
@@ -165,9 +165,6 @@
     def z_up(k):
         return lax.rem(z + k, depth)
 
-    def z_down(k):
-        return lax.rem(z + depth - k, depth)
-
     core_peer = expert_at(z, y, other_c)
     y_peer = expert_at(z, other_y, c)
 
@@ -206,13 +203,27 @@
     def slot(layer, batch):
         return layer * batches + batch
 
-    def gather_core(s, yy, zz, number):
-        block = rows.at[s, c, yy, zz]
-        return remote(block, block, ac_s.at[s, number], ac_r.at[s, number], core_peer)
-
-    def gather_y(s, zz, number):
-        block = rows.at[s, c, y, zz]
-        return remote(block, block, ay_s.at[s, number], ay_r.at[s, number], y_peer)
+    def nearest(n):
+        chosen = z * 0
+        for at in range(depth):
+            ranked = sorted(range(depth), key=lambda v: (abs(v - at), v))
+            chosen = jnp.where(z == at, ranked[n], chosen)
+        return chosen
+
+    near = [z] + [nearest(n) for n in range(1, depth)]
+
+    def row_block(s, cc, yy, zz):
+        if s == 0:
+            return rows.at[s, cc, yy, zz]
+        return rows.at[s, cc, yy, zz, :, pl.ds(0, features)]
+
+    def gather_core(s, cc, yy, zz):
+        block = row_block(s, cc, yy, zz)
+        return remote(block, block, ac_s.at[s, yy, zz], ac_r.at[s, yy, zz], core_peer)
+
+    def gather_y(s, yy, zz):
+        block = row_block(s, c, yy, zz)
+        return remote(block, block, ay_s.at[s, zz], ay_r.at[s, zz], y_peer)
 
     def norm_send(layer, batch):
         s = slot(layer, batch)
@@ -220,62 +231,67 @@
         scale = lax.rsqrt(jnp.mean(h * h, axis=-1, keepdims=True) + eps)
         normed = (h * scale * gain_ref[pl.ds(layer, 1), :]).astype(jnp.bfloat16)
         rows[s, c, y, z, :, pl.ds(0, features)] = normed
-        lanes = lax.broadcasted_iota(jnp.int32, (tokens, LANES), 1)
-        chosen = routes_ref[layer, batch]
-        named = jnp.zeros((tokens, LANES), jnp.float32)
-        for k in range(chosen.shape[1]):
-            named = named + (chosen[:, k : k + 1] == lanes).astype(jnp.float32)
-        rows[s, c, y, z, :, pl.ds(features, LANES)] = named.astype(jnp.bfloat16)
-        block = rows.at[s, c, y, z]
-        for k in range(1, depth):
-            go(remote(block, block, az_s.at[s, k - 1], az_r.at[s, k - 1], expert_at(z_up(k), y, c)))
-        go(gather_y(s, z, 0))
-        go(gather_core(s, y, z, 0))
-
-    def gather_z_done(layer, batch):
-        s = slot(layer, batch)
-        for k in range(1, depth):
-            zz = z_down(k)
-            block = rows.at[s, c, y, zz]
-            remote(block, block, az_s.at[s, k - 1], az_r.at[s, k - 1], y_peer).wait_recv()
-            go(gather_y(s, zz, k))
-            go(gather_core(s, y, zz, k))
-
-    def gather_y_done(layer, batch):
-        s = slot(layer, batch)
-        for k in range(depth):
-            zz = z_down(k)
-            block = rows.at[s, c, other_y, zz]
-            remote(block, block, ay_s.at[s, k], ay_r.at[s, k], y_peer).wait_recv()
-            go(gather_core(s, other_y, zz, depth + k))
+        if s == 0:
+            lanes = lax.broadcasted_iota(jnp.int32, (tokens, LANES), 1)
+            named = jnp.zeros((tokens, LANES), jnp.float32)
+            for lay in range(layers):
+                for bat in range(batches):
+                    chosen = routes_ref[lay, bat] + slot(lay, bat) * count
+                    for k in range(chosen.shape[1]):
+                        named = named + (chosen[:, k : k + 1] == lanes).astype(jnp.float32)
+            rows[s, c, y, z, :, pl.ds(features, LANES)] = named.astype(jnp.bfloat16)
+        block = row_block(s, c, y, z)
+        for n in range(1, depth):
+            go(remote(block, block, az_s.at[s, near[n]], az_r.at[s, z], expert_at(near[n], y, c)))
+        go(gather_y(s, y, z))
+        go(gather_core(s, c, y, z))
+
+    def gather_z_step(layer, batch, n):
+        s = slot(layer, batch)
+        zz = near[n]
+        block = row_block(s, c, y, zz)
+        remote(block, block, az_s.at[s, zz], az_r.at[s, zz], y_peer).wait_recv()
+        go(gather_y(s, y, zz))
+        go(gather_core(s, c, y, zz))
+
+    def gather_y_step(layer, batch, n):
+        s = slot(layer, batch)
+        gather_y(s, other_y, near[n]).wait_recv()
+        go(gather_core(s, c, other_y, near[n]))
 
     def gather_core_done(layer, batch):
         s = slot(layer, batch)
-        for number in range(PAIR * depth):
-            zz = z_down(number % depth)
-            block = rows.at[s, other_c, y if number < depth else other_y, zz]
-            remote(block, block, ac_s.at[s, number], ac_r.at[s, number], core_peer).wait_recv()
-
-    def compute(layer, batch):
+        for yy in (y, other_y):
+            for n in range(depth):
+                gather_core(s, other_c, yy, near[n]).wait_recv()
+
+    def compute(layer, batch, jobs):
         s = slot(layer, batch)
         if batch == 0:
             for load in loads[layer * 2 : layer * 2 + 2]:
                 load.wait()
-        named = flat_rows(rows[s, :, :, :, :, pl.ds(features, LANES)]).astype(jnp.float32)
+        named = flat_rows(rows[0, :, :, :, :, pl.ds(features, LANES)]).astype(jnp.float32)
         lanes = lax.broadcasted_iota(jnp.int32, named.shape, 1)
-        mine = jnp.sum(jnp.where(lanes == me, named, 0.0), axis=1, keepdims=True) > 0.5
-
-        def up_tile(j, carry):
-            gate_cols = pl.ds(pl.multiple_of(j * TILE, TILE), TILE)
-            up_cols = pl.ds(pl.multiple_of(units + j * TILE, TILE), TILE)
+        mine = jnp.sum(jnp.where(lanes == me + s * count, named, 0.0), axis=1, keepdims=True) > 0.5
+        ups, downs = units // TILE, features // TILE
+        points = ups + 2
+
+        def run_jobs(point):
+            for number, job in enumerate(jobs):
+                if number * points // len(jobs) == point:
+                    job()
+
+        for j in range(ups):
             x = flat_rows(rows[s, :, :, :, :, pl.ds(0, features)])
-            gate = jnp.dot(x, gu[layer, :, gate_cols], preferred_element_type=jnp.float32)
-            up = jnp.dot(x, gu[layer, :, up_cols], preferred_element_type=jnp.float32)
+            gate = jnp.dot(
+                x, gu[layer, :, pl.ds(j * TILE, TILE)], preferred_element_type=jnp.float32
+            )
+            up = jnp.dot(
+                x, gu[layer, :, pl.ds(units + j * TILE, TILE)], preferred_element_type=jnp.float32
+            )
             value = gate / (1.0 + jnp.exp(-gate)) * up
-            hidden[:, gate_cols] = jnp.where(mine, value, 0.0).astype(jnp.bfloat16)
-            return carry
-
-        lax.fori_loop(0, units // TILE, up_tile, 0)
+            hidden[:, pl.ds(j * TILE, TILE)] = jnp.where(mine, value, 0.0).astype(jnp.bfloat16)
+            run_jobs(j)
 
         def down_tile(j, carry):
             cols = pl.ds(pl.multiple_of(j * TILE, TILE), TILE)
@@ -285,105 +301,109 @@
             )
             return carry
 
-        lax.fori_loop(0, features // TILE, down_tile, 0)
-
-    def sum_core_copy(s, yy, number):
+        lax.fori_loop(0, downs // 2, down_tile, 0)
+        run_jobs(ups)
+        lax.fori_loop(downs // 2, downs, down_tile, 0)
+        run_jobs(ups + 1)
+
+    def sum_core_copy(s, cc, yy):
         return remote(
-            made.at[s, other_c, yy],
-            from_core.at[s, yy],
-            rc_s.at[s, number],
-            rc_r.at[s, number],
-            core_peer,
+            made.at[s, cc, yy], from_core.at[s, yy], rc_s.at[s, yy], rc_r.at[s, yy], core_peer
         )
 
     def sum_core(layer, batch):
         s = slot(layer, batch)
-        go(sum_core_copy(s, other_y, 0))
-        go(sum_core_copy(s, y, 1))
-
-    def sum_core_wait(s, yy, number):
-        block = from_core.at[s, yy]
-        remote(block, block, rc_s.at[s, number], rc_r.at[s, number], core_peer).wait_recv()
+        go(sum_core_copy(s, other_c, other_y))
+        go(sum_core_copy(s, other_c, y))
 
     def pair_sum(s, yy, zz):
         return made[s, c, yy, zz].astype(jnp.float32) + from_core[s, yy, zz].astype(jnp.float32)
 
+    def sum_y_copy(s, zz):
+        return remote(to_y.at[s, zz], from_y.at[s, zz], ry_s.at[s, zz], ry_r.at[s, zz], y_peer)
+
     def sum_y(layer, batch):
         s = slot(layer, batch)
-        sum_core_wait(s, other_y, 0)
-        for k in list(range(1, depth)) + [0]:
-            zz = z_up(k)
-            to_y[s, k] = pair_sum(s, other_y, zz).astype(jnp.bfloat16)
-            go(remote(to_y.at[s, k], from_y.at[s, k], ry_s.at[s, k], ry_r.at[s, k], y_peer))
-
-    def sum_y_wait(s, k):
-        remote(from_y.at[s, k], from_y.at[s, k], ry_s.at[s, k], ry_r.at[s, k], y_peer).wait_recv()
-
-    def sum_z(layer, batch):
-        s = slot(layer, batch)
-        sum_core_wait(s, y, 1)
-        for k in range(1, depth):
-            zz = z_up(k)
-            sum_y_wait(s, k)
-            total = pair_sum(s, y, zz) + from_y[s, k].astype(jnp.float32)
-            to_z[s, k - 1] = total.astype(jnp.bfloat16)
-            go(
-                remote(
-                    to_z.at[s, k - 1],
-                    from_z.at[s, k - 1],
-                    rz_s.at[s, k - 1],
-                    rz_r.at[s, k - 1],
-                    expert_at(zz, y, c),
-                )
+        sum_core_copy(s, other_c, other_y).wait_recv()
+        for n in reversed(range(depth)):
+            zz = near[n]
+            to_y[s, zz] = pair_sum(s, other_y, zz).astype(jnp.bfloat16)
+            go(sum_y_copy(s, zz))
+        sum_core_copy(s, other_c, y).wait_recv()
+
+    def sum_z_step(layer, batch, n):
+        s = slot(layer, batch)
+        zz = near[n]
+        sum_y_copy(s, zz).wait_recv()
+        total = pair_sum(s, y, zz) + from_y[s, zz].astype(jnp.float32)
+        to_z[s, zz] = total.astype(jnp.bfloat16)
+        go(
+            remote(
+                to_z.at[s, zz], from_z.at[s, z], rz_s.at[s, zz], rz_r.at[s, z], expert_at(zz, y, c)
             )
+        )
 
     def finish(layer, batch):
         s = slot(layer, batch)
-        sum_y_wait(s, 0)
-        total = pair_sum(s, y, z) + from_y[s, 0].astype(jnp.float32)
-        for k in range(depth - 1):
-            block = from_z.at[s, k]
-            remote(block, block, rz_s.at[s, k], rz_r.at[s, k], y_peer).wait_recv()
-            total = total + from_z[s, k].astype(jnp.float32)
+        sum_y_copy(s, z).wait_recv()
+        total = pair_sum(s, y, z) + from_y[s, z].astype(jnp.float32)
+        for n in range(1, depth):
+            zz = near[n]
+            block = from_z.at[s, zz]
+            remote(block, block, rz_s.at[s, zz], rz_r.at[s, zz], y_peer).wait_recv()
+            total = total + from_z[s, zz].astype(jnp.float32)
         h = (x_ref[batch] if layer == 0 else out_ref[layer - 1, batch]).astype(jnp.float32)
         out_ref[layer, batch] = (h + total * 0.125).astype(jnp.bfloat16)
 
+    def job(step, layer, batch, n=None):
+        if n is None:
+            return functools.partial(step, layer, batch)
+        return functools.partial(step, layer, batch, n)
+
+    def jobs_of(step, layer, batch, first):
+        return [job(step, layer, batch, n) for n in range(first, depth)]
+
+    def run(jobs):
+        for one in jobs:
+            one()
+
+    def mixed(left, right):
+        together = []
+        for number in range(max(len(left), len(right))):
+            together += left[number : number + 1] + right[number : number + 1]
+        return together
+
     norm_send(0, 0)
-    gather_z_done(0, 0)
+    run(jobs_of(gather_z_step, 0, 0, 1))
     norm_send(0, 1)
-    gather_y_done(0, 0)
-    gather_core_done(0, 0)
-    gather_z_done(0, 1)
-    compute(0, 0)
-    sum_core(0, 0)
-    gather_y_done(0, 1)
-    gather_core_done(0, 1)
-    sum_y(0, 0)
-    compute(0, 1)
-    sum_core(0, 1)
-    sum_z(0, 0)
-    sum_y(0, 1)
-    finish(0, 0)
-    norm_send(1, 0)
-    sum_z(0, 1)
-    gather_z_done(1, 0)
-    finish(0, 1)
-    norm_send(1, 1)
-    gather_y_done(1, 0)
-    gather_core_done(1, 0)
-    gather_z_done(1, 1)
-    compute(1, 0)
-    sum_core(1, 0)
-    gather_y_done(1, 1)
-    gather_core_done(1, 1)
-    sum_y(1, 0)
-    compute(1, 1)
-    sum_core(1, 1)
-    sum_z(1, 0)
-    sum_y(1, 1)
-    finish(1, 0)
-    sum_z(1, 1)
-    finish(1, 1)
+    run(jobs_of(gather_y_step, 0, 0, 0))
+    for layer in range(layers):
+        gather_core_done(layer, 0)
+        compute(
+            layer,
+            0,
+            jobs_of(gather_z_step, layer, 1, 1) + jobs_of(gather_y_step, layer, 1, 0)[:2],
+        )
+        sum_core(layer, 0)
+        sum_y(layer, 0)
+        run(jobs_of(gather_y_step, layer, 1, 2))
+        gather_core_done(layer, 1)
+        compute(layer, 1, list(reversed(jobs_of(sum_z_step, layer, 0, 1))))
+        sum_core(layer, 1)
+        finish(layer, 0)
+        if layer + 1 < layers:
+            norm_send(layer + 1, 0)
+        sum_y(layer, 1)
+        later = list(reversed(jobs_of(sum_z_step, layer, 1, 1)))
+        if layer + 1 < layers:
+            run(mixed(later, jobs_of(gather_z_step, layer + 1, 0, 1)))
+            gather_y_step(layer + 1, 0, 0)
+            finish(layer, 1)
+            norm_send(layer + 1, 1)
+            run(jobs_of(gather_y_step, layer + 1, 0, 1))
+        else:
+            run(later)
+            finish(layer, 1)
 
     for copy in sends:
         copy.wait_send()
@@ -399,7 +419,6 @@
     vmem = pl.BlockSpec(memory_space=pltpu.VMEM)
     hbm = pl.BlockSpec(memory_space=pl.ANY)
     dma = pltpu.SemaphoreType.DMA
-    short = max(depth - 1, 1)
     return pl.pallas_call(
         functools.partial(moe_kernel, count),
         out_shape=jax.ShapeDtypeStruct((layers, batches, tokens, features), bf16),
@@ -414,27 +433,36 @@
             pltpu.VMEM((slots, PAIR, depth, tokens, features), bf16),
             pltpu.VMEM((slots, depth, tokens, features), bf16),
             pltpu.VMEM((slots, depth, tokens, features), bf16),
-            pltpu.VMEM((slots, short, tokens, features), bf16),
-            pltpu.VMEM((slots, short, tokens, features), bf16),
+            pltpu.VMEM((slots, depth, tokens, features), bf16),
+            pltpu.VMEM((slots, depth, tokens, features), bf16),
             dma((layers, 2)),
-            dma((slots, short)),
-            dma((slots, short)),
-            dma((slots, depth)),
-            dma((slots, depth)),
-            dma((slots, PAIR * depth)),
-            dma((slots, PAIR * depth)),
-            dma((slots, 2)),
-            dma((slots, 2)),
-            dma((slots, depth)),
-            dma((slots, depth)),
-            dma((slots, short)),
-            dma((slots, short)),
+            dma((slots, depth)),
+            dma((slots, depth)),
+            dma((slots, depth)),
+            dma((slots, depth)),
+            dma((slots, PAIR, depth)),
+            dma((slots, PAIR, depth)),
+            dma((slots, PAIR)),
+            dma((slots, PAIR)),
+            dma((slots, depth)),
+            dma((slots, depth)),
+            dma((slots, depth)),
+            dma((slots, depth)),
         ],
         compiler_params=pltpu.CompilerParams(
             collective_id=0, has_side_effects=True, vmem_limit_bytes=60 << 20
         ),
         name="moe",
     )(inputs, routes, norm_gain, w_gate_up, w_down)
+
+
+def choose(count, inputs, routes, norm_gain, w_gate_up, w_down):
+    batches, tokens, features = inputs.shape
+    layers = routes.shape[0]
+    fits = layers == 2 and batches == 2 and layers * batches * count <= LANES
+    tiled = w_down.shape[2] % TILE == 0 and features % (2 * TILE) == 0 and tokens % 16 == 0
+    run = functools.partial(fused_on_device, count) if fits and tiled else on_device
+    return run(inputs, routes, norm_gain, w_gate_up, w_down)
 
 
 def solution(mesh):
@@ -446,9 +474,9 @@
         P("section", "expert", None, None),
     )
     count = mesh.shape["expert"]
-    fused = mesh.shape["section"] == 1 and count % (PAIR * PAIR) == 0 and PAIR * PAIR < count <= LANES
+    fused = mesh.shape["section"] == 1 and count % (PAIR * PAIR) == 0 and PAIR * PAIR < count
     return jax.shard_map(
-        functools.partial(fused_on_device, count) if fused else on_device,
+        functools.partial(choose, count) if fused else on_device,
         mesh=mesh,
         in_specs=placed,
         out_specs=P("section", None, ("groups", "expert"), None),

time: 89.8 us -> 85.3 us (0.950)
  Pallas kernels: 86.5 us -> 82 us
    pallas_call x1, Pallas kernels: 86.5 us -> 82 us  [fused_on_device(): pl.pallas_call(functools.partial(moe_kernel, count), out_shape=jax.ShapeD...]
where the time goes in v2:
time: 85.3 us; the launch traced here: 85 us
  Pallas kernels  82 us (96%)
  local copies, waits for them, and re-layouts  3.08 us (4%)
    pallas_call x1, Pallas kernels, fused_on_device(): pl.pallas_call(functools.partial(moe_kernel, count), out_shape=jax.ShapeD...  82 us
    unnamed x2, local copies, waits for them, and re-layouts  3.08 us

profile of v2, /device:TPU:0, one launch (start us, length us, event | category | flops | bytes accessed | tf_op | source)
XLA Modules:
  0.0 85.0 jit_solution(17495977726524460593)
XLA Ops:
  0.0 1.4 %copy.6.routes_ref = s32[2,2,16,8]{3,2,1,0:T(8,128)} copy(s32[2,2,16,8]{2,3,1,0:T(8,128)} %param.6) | data formatting | bytes 4096 | tf_op args[1]
  1.4 82.0 %moe.1 = bf16[2,2,16,2048]{3,2,1,0:T(8,128)(2,1)} custom-call(bf16[2,16,2048]{2,1,0:T(8,128)(2,1)} %x_ref.1, s32[2,2,16,8]{3,2,1,0:T(8,128)} %copy.6.routes_ref, f32[2,2048]{1,0:T(2,128)} %gain_ref.1, bf16[2,1,2048,1536]{3,2,1,0:T(8,128)(2,1)} %gu_hbm.1, bf16[2,1,768,2048]{3,2,1,0:T(8,128)(2,1)} %down_hbm.1), custom_call_target="tpu_custom_call" | custom-call | tf_op jit(solution)/shard_map/moe/pallas_call | solution.py:422
  83.4 1.7 %copy.8 = bf16[2,2,16,2048]{3,2,1,0:T(8,128)(2,1)} copy(bf16[2,2,16,2048]{3,2,1,0:T(8,128)(2,1)} %moe.1) | data formatting | bytes 524288
